TPU v7x, 32 devices: a whole 2x2x4 slice. The times are simulated.
32 devices in a mesh: groups: 2 (over y), qring: 4 (over x, core), kvring: 4 (over z), head: 1.
Axes of the slice: x: 2, y: 2, z: 4, core: 2. Of those that a mesh axis runs over, the one named last changes fastest.
Arguments:
- queries: bfloat16 [1536, 4096], P(('groups', 'qring', 'kvring'), 'head'), parts along dimension 0, may hold values from -6 to 6
- keys: bfloat16 [1536, 512], P(('groups', 'qring', 'kvring'), 'head'), parts along dimension 0, may hold values from -6 to 6
- values: bfloat16 [1536, 512], P(('groups', 'qring', 'kvring'), 'head'), parts along dimension 0, may hold values from -6 to 6
- doc_ids: int32 [1536], P('groups'), parts along dimension 0, may hold values from 0 to 15, never falling along the last dimension, each value on 1 to 480 neighbouring positions
- head_mask: int32 [32], P('head'), may hold values 0 or 1
- w_out: bfloat16 [4096, 8192], P('head', 'kvring'), may hold values from -0.5 to 0.5
Outputs:
- mixed: bfloat16 [1536, 8192], P(('groups', 'qring', 'head'), 'kvring'), parts along dimension 0
There are 2 independent parts, one for each index of `groups`. A program takes and returns all parts, laid end to end along the dimension named above; an argument that names none is the same for every part. Nothing has to cross between parts.
All inputs are finite; a program needn't handle non-finite values. No bound on the sum of `head_mask` on one device may be relied on, other than what follows from the above.
Results may differ from a plain program's by a relative error of at most 0.015.
Values may be sent and summed in bfloat16 or wider, within the bound.
A program may use at most 64 MiB of HBM per device.

v0:
```python
import math

import jax
import jax.numpy as jnp
from jax import lax
from jax.sharding import PartitionSpec as P

HD = 128


NEG = -1e30


def block_rows(total_rows, shard_rows):
    best_size = shard_rows
    for multiple in range(1, total_rows // shard_rows + 1):
        if total_rows // shard_rows % multiple == 0 and multiple * shard_rows <= 256:
            best_size = multiple * shard_rows
    return best_size


def attend_keys(state, visible, queries4, key_rows, value_rows, scale_factor):
    run_max, run_sum, run_out = state
    mask4 = visible[:, None, None, :]
    scores = (
        jnp.einsum("rgec,kgc->rgek", queries4, key_rows, preferred_element_type=jnp.float32)
        * scale_factor
    )
    scores = jnp.where(mask4, scores, NEG)
    new_max = jnp.maximum(run_max, jnp.max(scores, axis=-1))
    weights = jnp.where(mask4, jnp.exp(scores - new_max[..., None]), 0.0)
    shrink = jnp.exp(run_max - new_max)
    run_sum = run_sum * shrink + jnp.sum(weights, axis=-1)
    update = jnp.einsum(
        "rgek,kgc->rgec",
        weights.astype(jnp.bfloat16),
        value_rows,
        preferred_element_type=jnp.float32,
    )
    run_out = run_out * shrink[..., None] + update
    return (new_max, run_sum, run_out)


def fold_piece(
    state, pieces, key_start, queries4, query_doc, query_pos, doc_ids, shard_rows, scale_factor
):
    key_all, value_all = pieces
    total_rows = key_all.shape[0]
    block_size = block_rows(total_rows, shard_rows)

    def one_block(index, carry):
        offset = index * block_size
        key_rows = lax.dynamic_slice_in_dim(key_all, offset, block_size, 0)
        value_rows = lax.dynamic_slice_in_dim(value_all, offset, block_size, 0)
        first = key_start + offset
        key_doc = lax.dynamic_slice_in_dim(doc_ids, first, block_size, 0)
        key_pos = first + jnp.arange(block_size, dtype=jnp.int32)
        visible = (query_doc[:, None] == key_doc[None, :]) & (
            key_pos[None, :] <= query_pos[:, None]
        )
        return attend_keys(carry, visible, queries4, key_rows, value_rows, scale_factor)

    return lax.fori_loop(0, total_rows // block_size, one_block, state)


def per_device(queries, keys, values, doc_ids, head_mask, w_out):
    shard_rows = queries.shape[0]
    kv_local = keys.shape[1] // HD
    q_local = queries.shape[1] // HD
    per_group = q_local // kv_local
    scale_factor = 1.0 / math.sqrt(HD)
    cycle_size = lax.axis_size("kvring")
    cycle_index = lax.axis_index("kvring")
    loop_index = lax.axis_index("qring")
    quarter = cycle_size * shard_rows
    key_rows = keys.reshape(shard_rows, kv_local, HD)
    value_rows = values.reshape(shard_rows, kv_local, HD)
    loop_size = lax.axis_size("qring")
    gathered = lax.all_gather(queries, "qring", axis=0, tiled=True)
    query_total = loop_size * shard_rows
    row_ids = jnp.arange(query_total, dtype=jnp.int32)
    query_pos = row_ids // shard_rows * quarter + cycle_index * shard_rows + row_ids % shard_rows
    queries4 = gathered.reshape(query_total, kv_local, per_group, HD)
    query_doc = jnp.take(doc_ids, query_pos)
    key_base = loop_index * quarter
    initial = (
        jnp.full((query_total, kv_local, per_group), NEG, jnp.float32),
        jnp.zeros((query_total, kv_local, per_group), jnp.float32),
        jnp.zeros((query_total, kv_local, per_group, HD), jnp.float32),
    )
    run_max, run_sum, run_out = fold_piece(
        initial,
        (
            lax.all_gather(key_rows, "kvring", axis=0, tiled=True),
            lax.all_gather(value_rows, "kvring", axis=0, tiled=True),
        ),
        key_base,
        queries4,
        query_doc,
        query_pos,
        doc_ids,
        shard_rows,
        scale_factor,
    )
    top = lax.pmax(run_max, "qring")
    factor = jnp.exp(run_max - top)
    numer, denom = (
        lax.psum_scatter(
            (run_out * factor[..., None]).astype(jnp.bfloat16),
            "qring",
            scatter_dimension=0,
            tiled=True,
        ).astype(jnp.float32),
        lax.psum_scatter(
            (run_sum * factor).astype(jnp.bfloat16), "qring", scatter_dimension=0, tiled=True
        ).astype(jnp.float32),
    )
    mask_f = head_mask.reshape(kv_local, per_group).astype(jnp.float32)
    attended = (
        (numer / denom[..., None] * mask_f[None, :, :, None])
        .astype(jnp.bfloat16)
        .reshape(shard_rows, q_local * HD)
    )
    partial_sum = jnp.dot(
        lax.all_gather(attended, "kvring", axis=0, tiled=True),
        w_out,
        preferred_element_type=jnp.float32,
    )
    return lax.psum_scatter(
        partial_sum.astype(jnp.bfloat16), "head", scatter_dimension=0, tiled=True
    )


def solution(mesh):
    placed = (
        P(("groups", "qring", "kvring"), "head"),
        P(("groups", "qring", "kvring"), "head"),
        P(("groups", "qring", "kvring"), "head"),
        P("groups"),
        P("head"),
        P("head", "kvring"),
    )
    return jax.shard_map(
        per_device,
        mesh=mesh,
        in_specs=placed,
        out_specs=P(("groups", "qring", "head"), "kvring"),
        check_vma=False,
    )
```

profile of v0, /device:TPU:0, one launch (start us, length us, event | category | flops | bytes accessed | tf_op | source)
XLA Modules:
  0.0 176.9 jit_solution(12851402233796282457)
XLA Ops:
  6.5 0.7 all-gather.3.cloned.1.call-update
  7.3 0.0 reduce-scatter.10.cloned.1.call-start
  7.3 0.8 dynamic_slice.8
  8.1 1.9 %gather_fusion = s32[192]{0:T(256)S(1)} fusion(s32[768]{0:T(1024)} %param.9, s32[1024]{0:T(1024)S(1)} %pad_clamp_fusion), kind=kCustom, calls=%fused_computation | custom fusion | bytes 2304 | tf_op jit(solution)/shard_map/jit(_take)/gather | solution.py:84
  10.1 15.5 %all_gather.12 = bf16[192,4,128]{2,0,1:T(8,128)(2,1)S(1)} all-gather(bf16[48,4,128]{2,0,1:T(8,128)(2,1)S(1)} %copy_bitcast_fusion.3), channel_id=1, replica_groups=mesh['groups'=2,'qring'=4,'kvring'=4,'head'=1] {'kvring'}, dimensions={0}, use_global_device_ids=true | all-gather | bytes 245760 | tf_op jit(solution)/shard_map/all_gather | solution.py:94
  25.5 0.8 copy_bitcast_fusion.2
  26.3 14.7 %all_gather.14 = bf16[192,4,128]{2,0,1:T(8,128)(2,1)} all-gather(bf16[48,4,128]{2,0,1:T(8,128)(2,1)S(1)} %copy_bitcast_fusion.2), channel_id=1, replica_groups=mesh['groups'=2,'qring'=4,'kvring'=4,'head'=1] {'kvring'}, dimensions={0}, use_global_device_ids=true | all-gather | bytes 245760 | tf_op jit(solution)/shard_map/all_gather | solution.py:95
  41.0 0.1 compare_and_fusion
  41.2 1.7 copy.37
  42.9 4.5 %fusion = (f32[192,4,8]{0,2,1:T(8,128)S(1)}, f32[4,192,192,8]{2,1,3,0:T(8,128)}) fusion(pred[192,192]{0,1:T(8,128)(4,1)S(1)} %compare_and_fusion, bf16[192,4,8,128]{3,2,1,0:T(8,128)(2,1)S(1)} %bitcast.68, bf16[192,4,128]{2,0,1:T(8,128)(2,1)S(1)} %all_gather.12), kind=kOutput, calls=%fused_computation.3 | convolution fusion | flops 305522688 | bytes 6549504 | tf_op jit(solution)/shard_map/while/body/eval_jaxpr/rgec,kgc->rgek/dot_general | solution.py:26
  47.4 10.3 %pmax.7 = f32[192,4,8]{0,2,1:T(8,128)S(1)} all-reduce(f32[192,4,8]{0,2,1:T(8,128)S(1)} %broadcast_maximum_fusion), channel_id=1, replica_groups=mesh['groups'=2,'qring'=4,'kvring'=4,'head'=1] {'qring'}, use_global_device_ids=true, to_apply=%region_1.2 | all-reduce | flops 6144 | bytes 49152 | tf_op jit(solution)/shard_map/pmax | solution.py:105
  57.7 4.6 %fusion.1 = (f32[192,4,8]{0,2,1:T(8,128)S(1)}, bf16[192,4,8,192]{0,3,2,1:T(8,128)(2,1)S(1)}) fusion(f32[4,192,192,8]{2,1,3,0:T(8,128)} %get-tuple-element.33, f32[192,4,8]{0,2,1:T(8,128)S(1)} %broadcast_maximum_fusion, pred[192,192]{0,1:T(8,128)(4,1)S(1)} %compare_and_fusion), kind=kLoop, calls=%fused_computation.4 | loop fusion | flops 7071744 | bytes 7163904 | tf_op jit(solution)/shard_map/while/body/eval_jaxpr/reduce_sum | solution.py:33
  62.3 0.9 copy.21
  63.2 0.9 copy.24
  64.2 3.9 %copy.23 = bf16[192,4,8,192]{3,2,0,1:T(8,128)(2,1)} copy(bf16[192,4,8,192]{0,3,2,1:T(8,128)(2,1)S(1)} %get-tuple-element.30) | data formatting | bytes 4718592 | tf_op jit(solution)/shard_map/while/body/eval_jaxpr/convert_element_type | solution.py:36
  68.1 0.7 copy.33
  68.8 0.0 reduce-scatter.8.cloned.1.call-start
  68.9 3.4 %fusion.4 = bf16[192,4,8,128]{3,2,0,1:T(8,128)(2,1)S(1)} fusion(bf16[192,4,8,192]{3,2,0,1:T(8,128)(2,1)} %copy.23, f32[192,4,8]{2,0,1:T(8,128)} %copy.24, f32[192,4,8]{2,0,1:T(8,128)} %copy.21, bf16[192,4,128]{2,0,1:T(8,128)(2,1)S(1)} %copy-done.1), kind=kOutput, calls=%fused_computation.8 | convolution fusion | flops 304349184 | bytes 4177920 | tf_op jit(solution)/shard_map/while/body/eval_jaxpr/rgek,kgc->rgec/dot_general | solution.py:34
  72.3 0.3 copy.29
  72.6 1.9 %copy.50 = bf16[24,8,32,128]{3,1,2,0:T(8,128)(2,1)} copy(bf16[24,8,32,128]{3,2,1,0:T(8,128)(2,1)S(1)} %bitcast.67) | data formatting | bytes 3145728
  74.5 0.2 all-gather.5.cloned.1.call-start
  74.7 0.1 convert_element_type.38
  74.8 14.9 %reduce-scatter.10.cloned.1.call-done = bf16[48,32]{1,0:T(8,128)(2,1)} async-done(((bf16[192,32]{1,0:T(8,128)(2,1)}), bf16[48,32]{1,0:T(8,128)(2,1)}) %reduce-scatter.10.cloned.1.call-update) | async-done | bytes 3088
  89.7 0.8 copy.34
  90.5 0.1 copy.25
  90.6 29.7 %reduce-scatter.8.cloned.1.call-done = bf16[48,4096]{1,0:T(8,128)(2,1)} async-done(((bf16[192,4096]{1,0:T(8,128)(2,1)}), bf16[48,4096]{1,0:T(8,128)(2,1)}) %reduce-scatter.8.cloned.1.call-update) | async-done | bytes 393232
  120.3 1.1 copy.39
  121.3 0.3 multiply_convert_fusion
  121.6 0.1 copy.26
  121.7 0.9 copy.51
  122.6 37.2 %all-gather.5.cloned.1.call-done = bf16[192,4096]{1,0:T(8,128)(2,1)} async-done(((bf16[48,4096]{1,0:T(8,128)(2,1)}), bf16[192,4096]{1,0:T(8,128)(2,1)}) %all-gather.5.cloned.1.call-update) | async-done | bytes 1572880 | tf_op jit(solution)/shard_map/all_gather | solution.py:125
  159.8 10.6 %convolution_convert_fusion = bf16[192,2048]{1,0:T(8,128)(2,1)} fusion(bf16[192,4096]{1,0:T(8,128)(2,1)} %all-gather.5.cloned.1.call-done, bf16[4096,2048]{1,0:T(8,128)(2,1)} %param.11), kind=kOutput, calls=%fused_computation.9 | convolution fusion | flops 3221618688 | bytes 19136512 | tf_op jit(solution)/shard_map/dot_general | solution.py:124
  (20 shorter events, 0.2 us)
Async XLA Ops:
  6.5 3.5 %copy-start = (bf16[48,512]{1,0:T(8,128)(2,1)S(1)}, bf16[48,512]{1,0:T(8,128)(2,1)}, u32[]{:S(2)}) copy-start(bf16[48,512]{1,0:T(8,128)(2,1)} %param.7) | copy-start | bytes 147460
  6.5 34.6 %all-gather.3.cloned.1.call-start = ((), (), s32[]{:S(2)}) async-start(), calls=%async_computation.2 | async-start | bytes 1966080 | tf_op jit(solution)/shard_map/all_gather | solution.py:79
  7.3 82.5 %reduce-scatter.10.cloned.1.call-start = ((), (), s32[]{:S(2)}) async-start(), calls=%async_computation.5 | async-start | bytes 61440
  64.2 4.7 %copy-start.1 = (bf16[192,4,128]{2,0,1:T(8,128)(2,1)S(1)}, bf16[192,4,128]{2,0,1:T(8,128)(2,1)}, u32[]{:S(2)}) copy-start(bf16[192,4,128]{2,0,1:T(8,128)(2,1)} %all_gather.14) | copy-start | bytes 589828
  68.8 51.4 %reduce-scatter.8.cloned.1.call-start = ((), (), s32[]{:S(2)}) async-start(), calls=%async_computation.4 | async-start | bytes 1966080
  72.5 2.1 %copy-start.2 = (s32[32]{0:T(128)S(1)}, s32[32]{0:T(128)}, u32[]{:S(2)}) copy-start(s32[32]{0:T(128)} %param.10) | copy-start | bytes 388
  74.5 85.4 %all-gather.5.cloned.1.call-start = ((), (), s32[]{:S(2)}) async-start(), calls=%async_computation.3 | async-start | bytes 1966080 | tf_op jit(solution)/shard_map/all_gather | solution.py:125
Sparse Core Ops, SparseCore 0:
  8.9 22.3 all-gather.2
  69.0 20.7 reduce-scatter.9
  92.2 27.9 reduce-scatter.7
  122.8 37.0 all-gather.4
where the time goes:
time: 177 us
  waiting for transfers between devices  82.6 us (47%)
  blocking collectives  40.4 us (23%)
  matrix products  18.4 us (10%)
  local copies, waits for them, and re-layouts  16.9 us (10%)
  between operations  13.3 us (8%)
  other arithmetic  5.11 us (3%)
    unnamed x6, waiting for transfers between devices  45.4 us
    all_gather x1, waiting for transfers between devices, per_device(): lax.all_gather(attended, 'kvring', axis=0, tiled=True)  37.2 us
    all_gather x1, blocking collectives, per_device(): lax.all_gather(key_rows, 'kvring', axis=0, tiled=True)  15.5 us
    all_gather x1, blocking collectives, per_device(): lax.all_gather(value_rows, 'kvring', axis=0, tiled=True)  14.7 us
    dot_general x1, matrix products, per_device(): jnp.dot(lax.all_gather(attended, 'kvring', axis=0, tiled=True), w_out, pr...  10.6 us
    pmax x1, blocking collectives, per_device(): top = lax.pmax(run_max, 'qring')  10.3 us
    unnamed x13, local copies, waits for them, and re-layouts  7.34 us
    reduce_sum x1, other arithmetic, attend_keys(): run_sum = run_sum * shrink + jnp.sum(weights, axis=-1)  4.63 us
  transfers between devices with their start and end apart: 4, of which 3 were waited for; matrix products, arithmetic and copies ran while one was open for 6% of the time, Pallas kernels for 0%

commit v1 on v0

--- a/solution.py
+++ b/solution.py
@@ -1,8 +1,11 @@
+import functools
 import math
 
 import jax
 import jax.numpy as jnp
 from jax import lax
+from jax.experimental import pallas as pl
+from jax.experimental.pallas import tpu as pltpu
 from jax.sharding import PartitionSpec as P
 
 HD = 128
@@ -131,7 +134,316 @@
     )
 
 
+LINE = 4
+CHUNKS = 8
+
+
+def fused_kernel(
+    rings,
+    chunks,
+    per_group,
+    doc_ref,
+    mask_ref,
+    q_hbm,
+    k_hbm,
+    v_hbm,
+    w_hbm,
+    o_ref,
+    q_all,
+    k_all,
+    v_all,
+    w_all,
+    attended,
+    bias,
+    total,
+    local_sem,
+    w_sem,
+    kv_send,
+    kv_recv,
+    pass_send,
+    q_send,
+    q_recv,
+):
+    z = lax.axis_index("kvring")
+    q = lax.axis_index("qring")
+    shard = q_hbm.shape[0]
+    rows = LINE * shard
+    seq = k_all.shape[0]
+    width = q_hbm.shape[1] // chunks
+    per_chunk = width // HD
+    scale2 = math.log2(math.e) / math.sqrt(HD)
+    order = (2, 1, 3)
+    peers = tuple(range(1, rings))
+
+    def other(step):
+        return lax.rem(z + step, LINE)
+
+    def ring(step):
+        return lax.rem(q + step, rings)
+
+    def far(step):
+        gap = z - other(step)
+        return (gap == LINE - 1) | (gap == 1 - LINE)
+
+    def near(step):
+        return jnp.logical_not(far(step))
+
+    middle = (z == 1) | (z == 2)
+    relay_to = 3 * (z - 1)
+
+    def kv_rows(ring_at, line_at):
+        return pl.ds(pl.multiple_of((ring_at * LINE + line_at) * shard, 16), shard)
+
+    def q_rows(line_at):
+        return pl.ds(pl.multiple_of(line_at * shard, 16), shard)
+
+    def q_cols(c):
+        return pl.ds(pl.multiple_of(c * width, 128), width)
+
+    def kv_copies(from_input, line_at, sends, target):
+        at = kv_rows(q, line_at)
+        slot = q * LINE + line_at
+        out = []
+        for i, (own, everyone) in enumerate(((k_hbm, k_all), (v_hbm, v_all))):
+            out.append(
+                pltpu.make_async_remote_copy(
+                    src_ref=own if from_input else everyone.at[at],
+                    dst_ref=everyone.at[at],
+                    send_sem=sends.at[i],
+                    recv_sem=kv_recv.at[slot, i],
+                    device_id=target,
+                    device_id_type=pl.DeviceIdType.MESH,
+                )
+            )
+        return out
+
+    def kv_arrival(ring_at, line_at):
+        at = kv_rows(ring_at, line_at)
+        slot = ring_at * LINE + line_at
+        for i, everyone in enumerate((k_all, v_all)):
+            pltpu.make_async_remote_copy(
+                src_ref=everyone.at[at],
+                dst_ref=everyone.at[at],
+                send_sem=kv_send.at[0, i],
+                recv_sem=kv_recv.at[slot, i],
+                device_id={"kvring": other(1)},
+                device_id_type=pl.DeviceIdType.MESH,
+            ).wait_recv()
+
+    def q_copy(from_input, line_at, c, step, target):
+        place = q_all.at[q_rows(line_at), q_cols(c)]
+        return pltpu.make_async_remote_copy(
+            src_ref=q_hbm.at[:, q_cols(c)] if from_input else place,
+            dst_ref=place,
+            send_sem=q_send.at[step, c],
+            recv_sem=q_recv.at[line_at, c],
+            device_id={"kvring": target},
+            device_id_type=pl.DeviceIdType.MESH,
+        )
+
+    def w_copy(c):
+        at = pl.ds(pl.multiple_of(c * width, 128), width)
+        return pltpu.make_async_copy(w_hbm.at[at], w_all.at[at], w_sem.at[c])
+
+    local = [
+        pltpu.make_async_copy(q_hbm, q_all.at[q_rows(z)], local_sem.at[0]),
+        pltpu.make_async_copy(k_hbm, k_all.at[kv_rows(q, z)], local_sem.at[1]),
+        pltpu.make_async_copy(v_hbm, v_all.at[kv_rows(q, z)], local_sem.at[2]),
+    ]
+
+    barrier = pltpu.get_barrier_semaphore()
+    for step in order:
+
+        @pl.when(near(step))
+        def _(step=step):
+            pl.semaphore_signal(
+                barrier, inc=1, device_id={"kvring": other(step)}, device_id_type=pl.DeviceIdType.MESH
+            )
+
+    for step in peers:
+        pl.semaphore_signal(
+            barrier, inc=1, device_id={"qring": ring(step)}, device_id_type=pl.DeviceIdType.MESH
+        )
+    for copy in local:
+        copy.start()
+
+    @pl.loop(0, chunks)
+    def _(c):
+        w_copy(c).start()
+
+    @pl.when(middle)
+    def _():
+        pl.semaphore_wait(barrier, LINE - 1 + len(peers))
+
+    @pl.when(jnp.logical_not(middle))
+    def _():
+        pl.semaphore_wait(barrier, LINE - 2 + len(peers))
+
+    def send_kv_on(from_input, line_at, place):
+        for i, step in enumerate(peers):
+            for copy in kv_copies(from_input, line_at, pass_send.at[place, i], {"qring": ring(step)}):
+                copy.start()
+
+    def send_q(first, last):
+        @pl.loop(first, last)
+        def _(c):
+            for step in order:
+
+                @pl.when(near(step))
+                def _(step=step):
+                    q_copy(True, z, c, step, other(step)).start()
+
+    for step in order:
+
+        @pl.when(near(step))
+        def _(step=step):
+            for copy in kv_copies(True, z, kv_send.at[step], {"kvring": other(step)}):
+                copy.start()
+
+    send_kv_on(True, z, 0)
+    quota = chunks // LINE
+    send_q(0, quota)
+    for i, step in enumerate(order):
+        kv_arrival(q, other(step))
+        if step == 2:
+
+            @pl.when(middle)
+            def _():
+                for copy in kv_copies(False, other(2), kv_send.at[0], {"kvring": relay_to}):
+                    copy.start()
+
+        send_kv_on(False, other(step), step)
+        send_q((i + 1) * quota, (i + 2) * quota)
+
+    def q_arrival(step, c):
+        q_copy(False, other(step), c, 0, other(1)).wait_recv()
+
+    def relay(c):
+        q_arrival(2, c)
+
+        @pl.when(middle)
+        def _():
+            q_copy(False, other(2), c, 0, relay_to).start()
+
+    relay(0)
+
+    row_at = q * rows + lax.broadcasted_iota(jnp.int32, (rows, seq), 0)
+    key_at = lax.broadcasted_iota(jnp.int32, (rows, seq), 1)
+    key_doc = jnp.broadcast_to(doc_ref[...], (rows, seq))
+    row_doc = jnp.sum(jnp.where(row_at == key_at, key_doc, 0), axis=1, keepdims=True)
+    bias[...] = jnp.where((key_doc == row_doc) & (key_at <= row_at), 0.0, NEG)
+    total[...] = jnp.zeros_like(total)
+
+    for copy in local:
+        copy.wait()
+    for step in peers:
+        for line_at in range(LINE):
+            kv_arrival(ring(step), line_at)
+
+    @pl.loop(0, chunks)
+    def _(c):
+        for step in (1, 3):
+            q_arrival(step, c)
+        kv_head = c * per_chunk // per_group
+        kv_cols = pl.ds(pl.multiple_of(kv_head * HD, 128), HD)
+        for e in range(per_chunk):
+            head = c * per_chunk + e
+            queries = q_all[:, pl.ds(pl.multiple_of(head * HD, 128), HD)]
+            scores = lax.dot_general(
+                queries,
+                k_all[:, kv_cols],
+                (((1,), (1,)), ((), ())),
+                preferred_element_type=jnp.float32,
+            )
+            scores = scores * scale2 + bias[...]
+            top = jnp.max(scores, axis=-1, keepdims=True)
+            weights = jnp.exp2(scores - top)
+            denom = jnp.sum(weights, axis=-1, keepdims=True)
+            context = jnp.dot(
+                weights.astype(jnp.bfloat16), v_all[:, kv_cols], preferred_element_type=jnp.float32
+            )
+            keep = mask_ref[head].astype(jnp.float32)
+            attended[:, e * HD : (e + 1) * HD] = (context / denom * keep).astype(jnp.bfloat16)
+
+        @pl.when(c + 1 < chunks)
+        def _():
+            relay(c + 1)
+
+        w_copy(c).wait()
+        total[...] += jnp.dot(
+            attended[...],
+            w_all[pl.ds(pl.multiple_of(c * width, 128), width), :],
+            preferred_element_type=jnp.float32,
+        )
+
+    o_ref[...] = total[...].astype(jnp.bfloat16)
+
+    for step in order:
+
+        @pl.when(near(step))
+        def _(step=step):
+            for copy in kv_copies(True, z, kv_send.at[step], {"kvring": other(step)}):
+                copy.wait_send()
+
+            @pl.loop(0, chunks)
+            def _(c):
+                q_copy(True, z, c, step, other(step)).wait_send()
+
+    @pl.when(middle)
+    def _():
+        for copy in kv_copies(False, other(2), kv_send.at[0], {"kvring": relay_to}):
+            copy.wait_send()
+
+        @pl.loop(0, chunks)
+        def _(c):
+            q_copy(False, other(2), c, 0, relay_to).wait_send()
+
+    for place in range(LINE):
+        for i, step in enumerate(peers):
+            for copy in kv_copies(place == 0, other(place), pass_send.at[place, i], {"qring": ring(step)}):
+                copy.wait_send()
+
+
+def fused_device(queries, keys, values, doc_ids, head_mask, w_out):
+    shard_rows = queries.shape[0]
+    rings = lax.axis_size("qring")
+    seq = doc_ids.shape[0]
+    rows = LINE * shard_rows
+    columns = w_out.shape[1]
+    width = queries.shape[1] // CHUNKS
+    per_group = queries.shape[1] // keys.shape[1]
+    vmem = pl.BlockSpec(memory_space=pltpu.VMEM)
+    anywhere = pl.BlockSpec(memory_space=pl.ANY)
+    dma = pltpu.SemaphoreType.DMA
+    return pl.pallas_call(
+        functools.partial(fused_kernel, rings, CHUNKS, per_group),
+        out_shape=jax.ShapeDtypeStruct((rows, columns), jnp.bfloat16),
+        in_specs=[vmem, pl.BlockSpec(memory_space=pltpu.SMEM), anywhere, anywhere, anywhere, anywhere],
+        out_specs=vmem,
+        scratch_shapes=[
+            pltpu.VMEM((rows, queries.shape[1]), jnp.bfloat16),
+            pltpu.VMEM((seq, keys.shape[1]), jnp.bfloat16),
+            pltpu.VMEM((seq, keys.shape[1]), jnp.bfloat16),
+            pltpu.VMEM(w_out.shape, jnp.bfloat16),
+            pltpu.VMEM((rows, width), jnp.bfloat16),
+            pltpu.VMEM((rows, seq), jnp.float32),
+            pltpu.VMEM((rows, columns), jnp.float32),
+            dma((3,)),
+            dma((CHUNKS,)),
+            dma((LINE, 2)),
+            dma((rings * LINE, 2)),
+            dma((LINE, rings - 1, 2)),
+            dma((LINE, CHUNKS)),
+            dma((LINE, CHUNKS)),
+        ],
+        compiler_params=pltpu.CompilerParams(
+            collective_id=0, has_side_effects=True, vmem_limit_bytes=48 * 1024 * 1024
+        ),
+    )(doc_ids.reshape(1, seq), head_mask, queries, keys, values, w_out)
+
+
 def solution(mesh):
+    small = mesh.shape["kvring"] == LINE and mesh.shape["head"] == 1
     placed = (
         P(("groups", "qring", "kvring"), "head"),
         P(("groups", "qring", "kvring"), "head"),
@@ -141,7 +453,7 @@
         P("head", "kvring"),
     )
     return jax.shard_map(
-        per_device,
+        fused_device if small else per_device,
         mesh=mesh,
         in_specs=placed,
         out_specs=P(("groups", "qring", "head"), "kvring"),

time: 177 us -> 51.8 us (0.29)
  waiting for transfers between devices: 82.6 us -> 0 us
  Pallas kernels: 0 us -> 46.7 us
  blocking collectives: 40.4 us -> 0 us
  matrix products: 18.4 us -> 0 us
  between operations: 13.3 us -> 0.01 us
  local copies, waits for them, and re-layouts: 16.9 us -> 4.82 us
  other arithmetic: 5.11 us -> 0 us
    pallas_call x0 -> x1, Pallas kernels: none -> 46.7 us  [fused_device(): pl.pallas_call(functools.partial(fused_kernel, rings, CHUNKS, per_group),...]
    unnamed x6 -> x0, waiting for transfers between devices: 45.4 us -> none
    all_gather x2 -> x0, waiting for transfers between devices: 37.2 us -> none  [the longest x1 37.2 us: per_device(): lax.all_gather(attended, 'kvring', axis=0, tiled=True)]
    all_gather x2 -> x0, blocking collectives: 30.1 us -> none  [the longest x1 15.5 us: per_device(): lax.all_gather(key_rows, 'kvring', axis=0, tiled=True)]
    dot_general x3 -> x0, matrix products: 18.4 us -> none  [the longest x1 10.6 us: per_device(): jnp.dot(lax.all_gather(attended, 'kvring', axis=0, tiled=True), w_out, pr...]
    pmax x1 -> x0, blocking collectives: 10.3 us -> none  [per_device(): top = lax.pmax(run_max, 'qring')]
    reduce_sum x1 -> x0, other arithmetic: 4.63 us -> none  [attend_keys(): run_sum = run_sum * shrink + jnp.sum(weights, axis=-1)]
    convert_element_type x4 -> x0, local copies, waits for them, and re-layouts: 4.18 us -> none  [the longest x1 3.94 us: attend_keys(): weights.astype(jnp.bfloat16)]
  transfers between devices with their start and end apart: 4 -> 0, of which waited for: 3 -> 0; matrix products, arithmetic and copies ran while one was open for 6% -> 0% of each run, Pallas kernels for 0% -> 0%
where the time goes in v1:
time: 51.8 us; the launch traced here: 51.5 us
  Pallas kernels  46.7 us (90%)
  local copies, waits for them, and re-layouts  4.82 us (9%)
    pallas_call x1, Pallas kernels, fused_device(): pl.pallas_call(functools.partial(fused_kernel, rings, CHUNKS, per_group),...  46.7 us
    unnamed x9, local copies, waits for them, and re-layouts  4.13 us

profile of v1, /device:TPU:0, one launch (start us, length us, event | category | flops | bytes accessed | tf_op | source)
XLA Modules:
  0.0 51.5 jit_solution(16100476738742971575)
XLA Ops:
  0.0 0.7 %reshape.3.doc_ref = s32[1,768]{1,0:T(1,128)S(1)} reshape(s32[768]{0:T(1024)} %param.9) | data formatting | bytes 6144 | tf_op jit(solution)/shard_map/reshape | solution.py:442
  0.7 0.0 copy-start
  0.7 1.0 %copy-done = bf16[48,4096]{1,0:T(8,128)(2,1)S(1)} copy-done((bf16[48,4096]{1,0:T(8,128)(2,1)S(1)}, bf16[48,4096]{1,0:T(8,128)(2,1)}, u32[]{:S(2)}) %copy-start) | copy-done | bytes 393240
  1.7 0.0 copy-start.1
  1.7 0.8 %copy-done.1 = bf16[48,512]{1,0:T(8,128)(2,1)S(1)} copy-done((bf16[48,512]{1,0:T(8,128)(2,1)S(1)}, bf16[48,512]{1,0:T(8,128)(2,1)}, u32[]{:S(2)}) %copy-start.1) | copy-done | bytes 49176
  2.5 0.0 copy-start.2
  2.5 0.8 %copy-done.2 = bf16[48,512]{1,0:T(8,128)(2,1)S(1)} copy-done((bf16[48,512]{1,0:T(8,128)(2,1)S(1)}, bf16[48,512]{1,0:T(8,128)(2,1)}, u32[]{:S(2)}) %copy-start.2) | copy-done | bytes 49176
  3.3 0.0 copy-start.3
  3.3 0.7 %copy-done.3 = s32[32]{0:T(128)S(1)} copy-done((s32[32]{0:T(128)S(1)}, s32[32]{0:T(128)}, u32[]{:S(2)}) %copy-start.3) | copy-done | bytes 152
  3.9 46.7 %shard_map.64 = bf16[192,2048]{1,0:T(8,128)(2,1)S(1)} custom-call(s32[1,768]{1,0:T(1,128)S(1)} %reshape.3.doc_ref, s32[32]{0:T(128)S(1)} %copy-done.3, bf16[48,4096]{1,0:T(8,128)(2,1)S(1)} %copy-done, bf16[48,512]{1,0:T(8,128)(2,1)S(1)} %copy-done.1, bf16[48,512]{1,0:T(8,128)(2,1)S(1)} %copy-done.2, bf16[4096,2048]{1,0:T(8,128)(2,1)} %w_hbm.1), custom_call_target="tpu_custom_call" | custom-call | tf_op jit(solution)/shard_map/pallas_call | solution.py:418
  50.6 0.9 %copy.8 = bf16[192,2048]{1,0:T(8,128)(2,1)} copy(bf16[192,2048]{1,0:T(8,128)(2,1)S(1)} %shard_map.64) | data formatting | bytes 1572864
Async XLA Ops:
  0.7 1.0 %copy-start = (bf16[48,4096]{1,0:T(8,128)(2,1)S(1)}, bf16[48,4096]{1,0:T(8,128)(2,1)}, u32[]{:S(2)}) copy-start(bf16[48,4096]{1,0:T(8,128)(2,1)} %q_hbm.1) | copy-start | bytes 1179652
  1.7 0.8 %copy-start.1 = (bf16[48,512]{1,0:T(8,128)(2,1)S(1)}, bf16[48,512]{1,0:T(8,128)(2,1)}, u32[]{:S(2)}) copy-start(bf16[48,512]{1,0:T(8,128)(2,1)} %k_hbm.1) | copy-start | bytes 147460
  2.5 0.8 %copy-start.2 = (bf16[48,512]{1,0:T(8,128)(2,1)S(1)}, bf16[48,512]{1,0:T(8,128)(2,1)}, u32[]{:S(2)}) copy-start(bf16[48,512]{1,0:T(8,128)(2,1)} %v_hbm.1) | copy-start | bytes 147460
  3.3 0.7 %copy-start.3 = (s32[32]{0:T(128)S(1)}, s32[32]{0:T(128)}, u32[]{:S(2)}) copy-start(s32[32]{0:T(128)} %mask_ref.1) | copy-start | bytes 388

commit v2 on v1

--- a/solution.py
+++ b/solution.py
@@ -136,19 +136,23 @@
 
 LINE = 4
 CHUNKS = 8
+RAW = 3
+RINGS = 4
+VMEM_LIMIT = 66200000
 
 
 def fused_kernel(
-    rings,
     chunks,
     per_group,
-    doc_ref,
-    mask_ref,
+    doc_hbm,
+    mask_hbm,
     q_hbm,
     k_hbm,
     v_hbm,
     w_hbm,
     o_ref,
+    doc_row,
+    mask_ref,
     q_all,
     k_all,
     v_all,
@@ -161,6 +165,7 @@
     kv_send,
     kv_recv,
     pass_send,
+    mate_send,
     q_send,
     q_recv,
 ):
@@ -173,13 +178,12 @@
     per_chunk = width // HD
     scale2 = math.log2(math.e) / math.sqrt(HD)
     order = (2, 1, 3)
-    peers = tuple(range(1, rings))
+    across = lax.rem(q + 2, RINGS)
+    mate = q + 1 - 2 * lax.rem(q, 2)
+    across_of_mate = lax.rem(mate + 2, RINGS)
 
     def other(step):
         return lax.rem(z + step, LINE)
-
-    def ring(step):
-        return lax.rem(q + step, rings)
 
     def far(step):
         gap = z - other(step)
@@ -200,9 +204,9 @@
     def q_cols(c):
         return pl.ds(pl.multiple_of(c * width, 128), width)
 
-    def kv_copies(from_input, line_at, sends, target):
-        at = kv_rows(q, line_at)
-        slot = q * LINE + line_at
+    def kv_copies(from_input, line_at, sends, target, ring_at=q):
+        at = kv_rows(ring_at, line_at)
+        slot = ring_at * LINE + line_at
         out = []
         for i, (own, everyone) in enumerate(((k_hbm, k_all), (v_hbm, v_all))):
             out.append(
@@ -251,6 +255,9 @@
         pltpu.make_async_copy(v_hbm, v_all.at[kv_rows(q, z)], local_sem.at[2]),
     ]
 
+    doc_copy = pltpu.make_async_copy(doc_hbm, doc_row, local_sem.at[3])
+    mask_copy = pltpu.make_async_copy(mask_hbm, mask_ref, local_sem.at[4])
+
     barrier = pltpu.get_barrier_semaphore()
     for step in order:
 
@@ -260,11 +267,11 @@
                 barrier, inc=1, device_id={"kvring": other(step)}, device_id_type=pl.DeviceIdType.MESH
             )
 
-    for step in peers:
+    for ring_at in (across, mate):
         pl.semaphore_signal(
-            barrier, inc=1, device_id={"qring": ring(step)}, device_id_type=pl.DeviceIdType.MESH
+            barrier, inc=1, device_id={"qring": ring_at}, device_id_type=pl.DeviceIdType.MESH
         )
-    for copy in local:
+    for copy in (doc_copy, mask_copy, *local):
         copy.start()
 
     @pl.loop(0, chunks)
@@ -273,25 +280,41 @@
 
     @pl.when(middle)
     def _():
-        pl.semaphore_wait(barrier, LINE - 1 + len(peers))
+        pl.semaphore_wait(barrier, LINE + 1)
 
     @pl.when(jnp.logical_not(middle))
     def _():
-        pl.semaphore_wait(barrier, LINE - 2 + len(peers))
+        pl.semaphore_wait(barrier, LINE)
 
     def send_kv_on(from_input, line_at, place):
-        for i, step in enumerate(peers):
-            for copy in kv_copies(from_input, line_at, pass_send.at[place, i], {"qring": ring(step)}):
+        for i, ring_at in enumerate((across, mate)):
+            for copy in kv_copies(from_input, line_at, pass_send.at[place, i], {"qring": ring_at}):
                 copy.start()
 
-    def send_q(first, last):
-        @pl.loop(first, last)
-        def _(c):
-            for step in order:
-
-                @pl.when(near(step))
-                def _(step=step):
-                    q_copy(True, z, c, step, other(step)).start()
+    def kv_to_mate(line_at, place):
+        return kv_copies(False, line_at, mate_send.at[place], {"qring": mate}, across)
+
+    def send_across_on(line_at, place):
+        kv_arrival(across, line_at)
+        for copy in kv_to_mate(line_at, place):
+            copy.start()
+
+    def send_q(from_input, c):
+        for step in order:
+
+            @pl.when(near(step))
+            def _(step=step):
+                q_copy(from_input, z, c, step, other(step)).start()
+
+    def q_arrival(step, c):
+        q_copy(False, other(step), c, 0, other(1)).wait_recv()
+
+    def relay(c):
+        q_arrival(2, c)
+
+        @pl.when(middle)
+        def _():
+            q_copy(False, other(2), c, 0, relay_to).start()
 
     for step in order:
 
@@ -301,8 +324,8 @@
                 copy.start()
 
     send_kv_on(True, z, 0)
-    quota = chunks // LINE
-    send_q(0, quota)
+    send_q(True, 0)
+    behind = (0,) + order
     for i, step in enumerate(order):
         kv_arrival(q, other(step))
         if step == 2:
@@ -313,67 +336,101 @@
                     copy.start()
 
         send_kv_on(False, other(step), step)
-        send_q((i + 1) * quota, (i + 2) * quota)
-
-    def q_arrival(step, c):
-        q_copy(False, other(step), c, 0, other(1)).wait_recv()
-
-    def relay(c):
-        q_arrival(2, c)
-
-        @pl.when(middle)
-        def _():
-            q_copy(False, other(2), c, 0, relay_to).start()
-
-    relay(0)
-
+        if i + 1 < RAW:
+            send_q(True, i + 1)
+        send_across_on(other(behind[i]), behind[i])
+
+    doc_copy.wait()
     row_at = q * rows + lax.broadcasted_iota(jnp.int32, (rows, seq), 0)
     key_at = lax.broadcasted_iota(jnp.int32, (rows, seq), 1)
-    key_doc = jnp.broadcast_to(doc_ref[...], (rows, seq))
+    key_doc = jnp.broadcast_to(doc_row[...].reshape(1, seq), (rows, seq))
     row_doc = jnp.sum(jnp.where(row_at == key_at, key_doc, 0), axis=1, keepdims=True)
     bias[...] = jnp.where((key_doc == row_doc) & (key_at <= row_at), 0.0, NEG)
-    total[...] = jnp.zeros_like(total)
-
+    send_across_on(other(3), 3)
+    relay(0)
+    mask_copy.wait()
     for copy in local:
         copy.wait()
-    for step in peers:
-        for line_at in range(LINE):
-            kv_arrival(ring(step), line_at)
-
-    @pl.loop(0, chunks)
+    for place in (0,) + order:
+        kv_arrival(mate, other(place))
+    for place in (0,) + order:
+        kv_arrival(across_of_mate, other(place))
+
+    def attend(queries, hidden, kv_head):
+        kv_cols = pl.ds(pl.multiple_of(kv_head * HD, 128), HD)
+        scores = lax.dot_general(
+            queries, k_all[:, kv_cols], (((1,), (1,)), ((), ())), preferred_element_type=jnp.float32
+        )
+        parts = queries.shape[0] // hidden.shape[0]
+        scores = (scores * scale2).reshape(parts, hidden.shape[0], seq) + hidden[None]
+        scores = scores.reshape(queries.shape[0], seq)
+        top = jnp.max(scores, axis=-1, keepdims=True)
+        weights = jnp.exp2(scores - top)
+        denom = jnp.sum(weights, axis=-1, keepdims=True)
+        context = jnp.dot(
+            weights.astype(jnp.bfloat16), v_all[:, kv_cols], preferred_element_type=jnp.float32
+        )
+        return context / denom
+
+    def head_cols(head):
+        return pl.ds(pl.multiple_of(head * HD, 128), HD)
+
+    @pl.loop(RAW, chunks)
     def _(c):
+        heads = [c * per_chunk + e for e in range(per_chunk)]
+        stacked = jnp.concatenate([q_all[q_rows(z), head_cols(head)] for head in heads], axis=0)
+        result = attend(stacked, bias[q_rows(z), :], c * per_chunk // per_group)
+        for e, head in enumerate(heads):
+            keep = mask_ref[head].astype(jnp.float32)
+            piece = result[e * shard : (e + 1) * shard] * keep
+            q_all[q_rows(z), head_cols(head)] = piece.astype(jnp.bfloat16)
+
+        @pl.when(c > RAW)
+        def _():
+            send_q(False, c - 1)
+
+        @pl.when(c - RAW + 1 < RAW)
+        def _():
+            relay(c - RAW + 1)
+
+    def weights_of(c):
+        w_copy(c).wait()
+        return w_all[pl.ds(pl.multiple_of(c * width, 128), width), :]
+
+    @pl.loop(0, RAW)
+    def _(c):
+        @pl.when(c == 0)
+        def _():
+            send_q(False, chunks - 1)
+
         for step in (1, 3):
             q_arrival(step, c)
-        kv_head = c * per_chunk // per_group
-        kv_cols = pl.ds(pl.multiple_of(kv_head * HD, 128), HD)
         for e in range(per_chunk):
             head = c * per_chunk + e
-            queries = q_all[:, pl.ds(pl.multiple_of(head * HD, 128), HD)]
-            scores = lax.dot_general(
-                queries,
-                k_all[:, kv_cols],
-                (((1,), (1,)), ((), ())),
-                preferred_element_type=jnp.float32,
-            )
-            scores = scores * scale2 + bias[...]
-            top = jnp.max(scores, axis=-1, keepdims=True)
-            weights = jnp.exp2(scores - top)
-            denom = jnp.sum(weights, axis=-1, keepdims=True)
-            context = jnp.dot(
-                weights.astype(jnp.bfloat16), v_all[:, kv_cols], preferred_element_type=jnp.float32
-            )
+            result = attend(q_all[:, head_cols(head)], bias[...], c * per_chunk // per_group)
             keep = mask_ref[head].astype(jnp.float32)
-            attended[:, e * HD : (e + 1) * HD] = (context / denom * keep).astype(jnp.bfloat16)
-
-        @pl.when(c + 1 < chunks)
-        def _():
-            relay(c + 1)
-
-        w_copy(c).wait()
+            attended[:, e * HD : (e + 1) * HD] = (result * keep).astype(jnp.bfloat16)
+        relay(c + RAW)
+        fresh = jnp.dot(attended[...], weights_of(c), preferred_element_type=jnp.float32)
+
+        @pl.when(c == 0)
+        def _():
+            total[...] = fresh
+
+        @pl.when(c > 0)
+        def _():
+            total[...] += fresh
+
+    @pl.loop(RAW, chunks)
+    def _(c):
+        @pl.when(c + RAW < chunks)
+        def _():
+            relay(c + RAW)
+
+        for step in (1, 3):
+            q_arrival(step, c)
         total[...] += jnp.dot(
-            attended[...],
-            w_all[pl.ds(pl.multiple_of(c * width, 128), width), :],
-            preferred_element_type=jnp.float32,
+            q_all[:, q_cols(c)], weights_of(c), preferred_element_type=jnp.float32
         )
 
     o_ref[...] = total[...].astype(jnp.bfloat16)
@@ -399,14 +456,15 @@
             q_copy(False, other(2), c, 0, relay_to).wait_send()
 
     for place in range(LINE):
-        for i, step in enumerate(peers):
-            for copy in kv_copies(place == 0, other(place), pass_send.at[place, i], {"qring": ring(step)}):
+        for i, ring_at in enumerate((across, mate)):
+            for copy in kv_copies(place == 0, other(place), pass_send.at[place, i], {"qring": ring_at}):
                 copy.wait_send()
+        for copy in kv_to_mate(other(place), place):
+            copy.wait_send()
 
 
 def fused_device(queries, keys, values, doc_ids, head_mask, w_out):
     shard_rows = queries.shape[0]
-    rings = lax.axis_size("qring")
     seq = doc_ids.shape[0]
     rows = LINE * shard_rows
     columns = w_out.shape[1]
@@ -416,11 +474,13 @@
     anywhere = pl.BlockSpec(memory_space=pl.ANY)
     dma = pltpu.SemaphoreType.DMA
     return pl.pallas_call(
-        functools.partial(fused_kernel, rings, CHUNKS, per_group),
+        functools.partial(fused_kernel, CHUNKS, per_group),
         out_shape=jax.ShapeDtypeStruct((rows, columns), jnp.bfloat16),
-        in_specs=[vmem, pl.BlockSpec(memory_space=pltpu.SMEM), anywhere, anywhere, anywhere, anywhere],
+        in_specs=[anywhere] * 6,
         out_specs=vmem,
         scratch_shapes=[
+            pltpu.VMEM((seq,), jnp.int32),
+            pltpu.SMEM(head_mask.shape, jnp.int32),
             pltpu.VMEM((rows, queries.shape[1]), jnp.bfloat16),
             pltpu.VMEM((seq, keys.shape[1]), jnp.bfloat16),
             pltpu.VMEM((seq, keys.shape[1]), jnp.bfloat16),
@@ -428,22 +488,24 @@
             pltpu.VMEM((rows, width), jnp.bfloat16),
             pltpu.VMEM((rows, seq), jnp.float32),
             pltpu.VMEM((rows, columns), jnp.float32),
-            dma((3,)),
+            dma((5,)),
             dma((CHUNKS,)),
             dma((LINE, 2)),
-            dma((rings * LINE, 2)),
-            dma((LINE, rings - 1, 2)),
+            dma((RINGS * LINE, 2)),
+            dma((LINE, 2, 2)),
+            dma((LINE, 2)),
             dma((LINE, CHUNKS)),
             dma((LINE, CHUNKS)),
         ],
         compiler_params=pltpu.CompilerParams(
-            collective_id=0, has_side_effects=True, vmem_limit_bytes=48 * 1024 * 1024
+            collective_id=0, has_side_effects=True, vmem_limit_bytes=VMEM_LIMIT
         ),
-    )(doc_ids.reshape(1, seq), head_mask, queries, keys, values, w_out)
+    )(doc_ids, head_mask, queries, keys, values, w_out)
 
 
 def solution(mesh):
-    small = mesh.shape["kvring"] == LINE and mesh.shape["head"] == 1
+    sizes = (mesh.shape["qring"], mesh.shape["kvring"], mesh.shape["head"])
+    small = sizes == (RINGS, LINE, 1)
     placed = (
         P(("groups", "qring", "kvring"), "head"),
         P(("groups", "qring", "kvring"), "head"),

time: 51.8 us -> 45.5 us (0.88)
  Pallas kernels: 46.7 us -> 43 us
  local copies, waits for them, and re-layouts: 4.82 us -> 2.09 us
    pallas_call x1, Pallas kernels: 46.7 us -> 43 us  [fused_device(): pl.pallas_call(functools.partial(fused_kernel, CHUNKS, per_group), out_sh...]
    unnamed x9 -> x1, local copies, waits for them, and re-layouts: 4.13 us -> 2.09 us
    reshape x1 -> x0, local copies, waits for them, and re-layouts: 0.69 us -> none  [fused_device(): doc_ids.reshape(1, seq)]
where the time goes in v2:
time: 45.5 us; the launch traced here: 45.1 us
  Pallas kernels  43 us (95%)
  local copies, waits for them, and re-layouts  2.09 us (5%)
    pallas_call x1, Pallas kernels, fused_device(): pl.pallas_call(functools.partial(fused_kernel, CHUNKS, per_group), out_sh...  43 us
    unnamed x1, local copies, waits for them, and re-layouts  2.09 us

profile of v2, /device:TPU:0, one launch (start us, length us, event | category | flops | bytes accessed | tf_op | source)
XLA Modules:
  0.0 45.1 jit_solution(10095748805950073258)
XLA Ops:
  0.0 43.0 %shard_map.64 = bf16[192,2048]{1,0:T(8,128)(2,1)} custom-call(s32[768]{0:T(1024)} %doc_hbm.1, s32[32]{0:T(128)} %mask_hbm.1, bf16[48,4096]{1,0:T(8,128)(2,1)} %q_hbm.1, bf16[48,512]{1,0:T(8,128)(2,1)} %k_hbm.1, bf16[48,512]{1,0:T(8,128)(2,1)} %v_hbm.1, bf16[4096,2048]{1,0:T(8,128)(2,1)} %w_hbm.1), custom_call_target="tpu_custom_call" | custom-call | tf_op jit(solution)/shard_map/pallas_call | solution.py:476
  43.0 2.1 %copy.8 = bf16[192,2048]{1,0:T(8,128)(2,1)} copy(bf16[192,2048]{1,0:T(8,128)(2,1)} %shard_map.64) | data formatting | bytes 1572864
